TPU v7x, 256 devices: a whole 4x4x8 slice. The times are simulated.
256 devices in a mesh: ens: 2 (over z_hi), tile: 128 (over x, y, z_lo, core).
Axes of the slice: x: 4, y: 4, z: 8 (z_hi: 2, z_lo: 4; z = z_hi * 4 + z_lo), core: 2. Of those that a mesh axis runs over, the one named last changes fastest.
Arguments:
- fields: bfloat16 [2, 128, 48, 48, 128], P('ens', 'tile'), may hold values from -6 to 6
- weight_first: bfloat16 [3, 3, 128, 128], replicated, may hold values from -0.1875 to 0.1875
- weight_second: bfloat16 [3, 3, 128, 128], replicated, may hold values from -0.1875 to 0.1875
- neighbours: int32 [128, 4], replicated, may hold values from 0 to 127, as said below
- cotangent: bfloat16 [2, 128, 48, 48, 128], P('ens', 'tile'), may hold values from -6 to 6
Outputs:
- out_field: bfloat16 [2, 128, 48, 48, 128], P('ens', 'tile')
- grad_fields: bfloat16 [2, 128, 48, 48, 128], P('ens', 'tile')
- grad_first: float32 [3, 3, 128, 128], replicated
- grad_second: float32 [3, 3, 128, 128], replicated
Inputs may be any that keep to these rules, and one draw needn't show every extreme that they name: The tiles form a grid of 8 rows of 16: the tile at index p has the four neighbours p - 16, p + 1, p + 16 and p - 1 modulo 128, one beside each side, listed clockwise from a starting side that varies from tile to tile; the relation is mutual.
All inputs are finite; a program needn't handle non-finite values.
Results may differ from a plain program's by a relative error of at most 0.0061.
Values may be sent and summed in bfloat16 or wider, within the bound.
A program may use at most 64 MiB of HBM per device.

v0:
```python
import jax
import jax.numpy as jnp
from jax import lax
from jax.experimental import pallas as pl
from jax.experimental.pallas import tpu as pltpu
from jax.sharding import PartitionSpec as P

MESH = pl.DeviceIdType.MESH
root_half = 0.7071067811865476
inv_root_tau = 0.3989422804014327
f32, bf16 = jnp.float32, jnp.bfloat16
S, C = 48, 128
PITCH = 64
SLOT = 64
OFFSETS = (1, -1, 16, -16)


TAPS = 5


class Place:
    def __init__(self):
        ens = lax.axis_index("ens")
        tile = lax.axis_index("tile")
        self.tile = tile
        self.core = tile % 2
        self.z = ens * 4 + (tile // 2) % 4
        self.q = tile // 8

    def device(self, q, z, core):
        return {"ens": z // 4, "tile": q * 8 + (z % 4) * 2 + core}


def greet(me):
    barrier = pltpu.get_barrier_semaphore()

    def signal(target):
        pl.semaphore_signal(barrier, inc=1, device_id=target, device_id_type=MESH)

    def plane(r, carry):
        signal(me.device((me.q + r) % 16, me.z, me.core))
        signal(me.device((me.q + r) % 16, me.z, 1 - me.core))
        return carry

    signal(me.device(me.q, me.z, 1 - me.core))
    lax.fori_loop(1, 16, plane, 0)

    def column(r, carry):
        signal(me.device(me.q, (me.z + r) % 8, me.core))
        return carry

    lax.fori_loop(1, 8, column, 0)
    for step in (1, -1):
        signal({"tile": (me.tile + step) % 128})
    return barrier


class Reduce:
    def __init__(self, me, grad, pair_out, pair_in, part, plane_in, column_in, whole, sems):
        self.me, self.grad = me, grad
        self.pair_out, self.pair_in, self.part = pair_out, pair_in, part
        self.plane_in, self.column_in, self.whole = plane_in, column_in, whole
        self.sems = sems

    def pair_copy(self):
        me = self.me
        return pltpu.make_async_remote_copy(
            src_ref=self.pair_out,
            dst_ref=self.pair_in,
            send_sem=self.sems.at[0, 0],
            recv_sem=self.sems.at[1, 0],
            device_id=me.device(me.q, me.z, 1 - me.core),
            device_id_type=MESH,
        )

    def plane_copy(self, target, source):
        return pltpu.make_async_remote_copy(
            src_ref=self.part.at[target],
            dst_ref=self.plane_in.at[source],
            send_sem=self.sems.at[0, 1 + target],
            recv_sem=self.sems.at[1, 1 + source],
            device_id=self.me.device(target, self.me.z, self.me.core),
            device_id_type=MESH,
        )

    def column_copy(self, target, source):
        return pltpu.make_async_remote_copy(
            src_ref=self.column_in.at[source],
            dst_ref=self.column_in.at[source],
            send_sem=self.sems.at[0, 17 + target],
            recv_sem=self.sems.at[1, 17 + source],
            device_id=self.me.device(self.me.q, target, self.me.core),
            device_id_type=MESH,
        )

    def whole_copy(self, target, target_core, source, source_core):
        return pltpu.make_async_remote_copy(
            src_ref=self.whole.at[source_core, source],
            dst_ref=self.whole.at[source_core, source],
            send_sem=self.sems.at[0, 25 + 16 * target_core + target],
            recv_sem=self.sems.at[1, 25 + 16 * source_core + source],
            device_id=self.me.device(target, self.me.z, target_core),
            device_id_type=MESH,
        )

    def send_pair(self):
        other = 1 - self.me.core
        for t in range(TAPS):
            self.pair_out[t] = self.grad[4 * other + t].astype(bf16)
        self.pair_copy().start()

    def send_plane(self):
        me = self.me
        self.pair_copy().wait_recv()

        def band(m, carry):
            rows = pl.ds(pl.multiple_of(16 * m, 16), 16)
            for t in range(TAPS):
                total = self.grad[4 * me.core + t, rows, :] + self.pair_in[t, rows, :].astype(f32)
                self.part[2 * m, t] = total[:8].astype(bf16)
                self.part[2 * m + 1, t] = total[8:].astype(bf16)
            return carry

        lax.fori_loop(0, 8, band, 0)
        self.plane_in[me.q] = self.part[me.q]

        def send(r, carry):
            self.plane_copy((me.q + r) % 16, me.q).start()
            return carry

        lax.fori_loop(1, 16, send, 0)

    def send_column(self):
        me = self.me

        def wait(r, carry):
            self.plane_copy((me.q + r) % 16, (me.q + r) % 16).wait_recv()
            return carry

        lax.fori_loop(1, 16, wait, 0)
        for t in range(TAPS):
            total = self.plane_in[0, t].astype(f32)
            for k in range(1, 16):
                total = total + self.plane_in[k, t].astype(f32)
            self.column_in[me.z, t] = total.astype(bf16)

        def send(r, carry):
            self.column_copy((me.z + r) % 8, me.z).start()
            return carry

        lax.fori_loop(1, 8, send, 0)

    def send_whole(self):
        me = self.me

        def wait(r, carry):
            self.column_copy((me.z + r) % 8, (me.z + r) % 8).wait_recv()
            return carry

        lax.fori_loop(1, 8, wait, 0)
        for t in range(TAPS):
            total = self.column_in[0, t].astype(f32)
            for k in range(1, 8):
                total = total + self.column_in[k, t].astype(f32)
            self.whole[me.core, me.q, t] = total.astype(bf16)

        def send(r, carry):
            target = (me.q + r) % 16
            self.whole_copy(target, me.core, me.q, me.core).start()
            self.whole_copy(target, 1 - me.core, me.q, me.core).start()
            return carry

        self.whole_copy(me.q, 1 - me.core, me.q, me.core).start()
        lax.fori_loop(1, 16, send, 0)

    def finish(self, out):
        me = self.me

        def wait(r, carry):
            source = (me.q + r) % 16
            self.whole_copy(source, me.core, source, me.core).wait_recv()
            self.whole_copy(source, 1 - me.core, source, 1 - me.core).wait_recv()
            return carry

        self.whole_copy(me.q, 1 - me.core, me.q, 1 - me.core).wait_recv()
        lax.fori_loop(1, 16, wait, 0)
        for tap in range(9):
            core = 0 if tap < TAPS else 1
            for k in range(16):
                out[tap, 8 * k : 8 * k + 8, :] = self.whole[core, k, tap - 4 * core].astype(
                    f32
                )

    def drain(self):
        me = self.me
        self.pair_copy().wait_send()

        def plane(r, carry):
            target = (me.q + r) % 16
            self.plane_copy(target, me.q).wait_send()
            self.whole_copy(target, me.core, me.q, me.core).wait_send()
            self.whole_copy(target, 1 - me.core, me.q, me.core).wait_send()
            return carry

        lax.fori_loop(1, 16, plane, 0)
        self.whole_copy(me.q, 1 - me.core, me.q, me.core).wait_send()

        def column(r, carry):
            self.column_copy((me.z + r) % 8, me.z).wait_send()
            return carry

        lax.fori_loop(1, 8, column, 0)


REDUCE_SCRATCH = [
    pltpu.VMEM((TAPS, 128, 128), bf16),
    pltpu.VMEM((TAPS, 128, 128), bf16),
    pltpu.VMEM((16, TAPS, 8, 128), bf16),
    pltpu.VMEM((16, TAPS, 8, 128), bf16),
    pltpu.VMEM((8, TAPS, 8, 128), bf16),
    pltpu.VMEM((2, 16, TAPS, 8, 128), bf16),
    pltpu.SemaphoreType.DMA((2, 57)),
]


class Swap:
    def __init__(self, me, outgoing, incoming, sems):
        self.me, self.outgoing, self.incoming, self.sems = me, outgoing, incoming, sems

    def copy(self, d):
        return pltpu.make_async_remote_copy(
            src_ref=self.outgoing.at[d, pl.ds(0, S)],
            dst_ref=self.incoming.at[d ^ 1, pl.ds(0, S)],
            send_sem=self.sems.at[0, d],
            recv_sem=self.sems.at[1, d ^ 1],
            device_id={"tile": (self.me.tile + OFFSETS[d]) % 128},
            device_id_type=MESH,
        )

    def send(self, strips, choose):
        routed = jnp.dot(choose[...], strips, preferred_element_type=f32).astype(bf16)
        for d in range(4):
            self.outgoing[d] = routed[SLOT * d : SLOT * d + SLOT]
        for d in range(4):
            self.copy(d).start()

    def receive(self, place):
        for d in range(4):
            self.copy(d).wait_recv()
        return jnp.dot(
            place[...], self.incoming[...].reshape(4 * SLOT, C), preferred_element_type=f32
        )

    def drain(self):
        for d in range(4):
            self.copy(d).wait_send()


def routing(me, neighbours, choose, place):
    sides = []
    for offset in OFFSETS:
        target = (me.tile + offset) % 128
        side = jnp.int32(0)
        for s in range(1, 4):
            side = side + jnp.where(neighbours[me.tile, s] == target, s, 0)
        sides.append(side)
    row = lax.broadcasted_iota(jnp.int32, (256, 256), 0)
    col = lax.broadcasted_iota(jnp.int32, (256, 256), 1)
    i, j = row % SLOT, col % SLOT
    inside = (i < S) & (j < S)
    same, flip = inside & (i == j), inside & (i + j == S - 1)

    def side_of(direction):
        out = jnp.full((256, 256), sides[0], jnp.int32)
        for d in range(1, 4):
            out = jnp.where(direction == d, sides[d], out)
        return out

    side = col // SLOT
    hit = (side_of(row // SLOT) == side) & (((side < 2) & same) | ((side >= 2) & flip))
    choose[...] = jnp.where(hit, 1.0, 0.0).astype(bf16)
    side = row // SLOT
    hit = (side_of(col // SLOT) == side) & (((side < 2) & flip) | ((side >= 2) & same))
    place[...] = jnp.where(hit, 1.0, 0.0).astype(bf16)


def edge_strips(padded, base):
    fill = jnp.zeros((SLOT - S, C), f32)

    def row(i):
        return padded[pl.ds(PITCH * (i + base) + 8, S), :]

    def column(j):
        return padded[pl.ds(PITCH * base + 8 + j, S, stride=PITCH), :]

    parts = []
    for strip in (row(0), column(S - 1), row(S - 1), column(0)):
        parts += [strip, fill]
    return jnp.concatenate(parts, axis=0).astype(bf16)


def spread(padded, base, wide, first, count):
    view = padded.reshape(padded.shape[0] // PITCH, PITCH, C)

    def body(k, carry):
        r = first + k
        for b in range(3):
            wide[r, :, C * b : C * b + C] = view[r + base, pl.ds(7 + b, S), :].astype(bf16)
        return carry

    lax.fori_loop(0, count, body, 0, unroll=4)


def fill_halo(padded, halo, wide):
    top, right, bottom, left = (halo[SLOT * s : SLOT * s + S] for s in range(4))
    padded[pl.ds(PITCH + 7, S, stride=PITCH), :] = left
    padded[pl.ds(PITCH + 56, S, stride=PITCH), :] = right
    padded[pl.ds(8, S), :] = top
    padded[pl.ds(PITCH * 49 + 8, S), :] = bottom
    padded[pl.ds(7, 1), :] = 0.5 * (top[:1] + left[:1])
    padded[pl.ds(56, 1), :] = 0.5 * (top[S - 1 :] + right[:1])
    padded[pl.ds(PITCH * 49 + 7, 1), :] = 0.5 * (left[S - 1 :] + bottom[:1])
    padded[pl.ds(PITCH * 49 + 56, 1), :] = 0.5 * (bottom[S - 1 :] + right[S - 1 :])
    view = padded.reshape(50, PITCH, C)
    for r in (0, 49):
        for b in range(3):
            wide[r, :, C * b : C * b + C] = view[r, pl.ds(7 + b, S), :].astype(bf16)

    def body(k, carry):
        r = 1 + k
        wide[r, :16, :C] = view[r, pl.ds(7, 16), :].astype(bf16)
        wide[r, 32:, 2 * C :] = view[r, pl.ds(41, 16), :].astype(bf16)
        return carry

    lax.fori_loop(0, S, body, 0, unroll=4)


def taps_of(wide, start):
    return jnp.concatenate(
        [wide[pl.ds(start + a, 8)].reshape(8 * S, 3 * C) for a in range(3)], axis=1
    )


def dot_rows(rows, weight):
    return lax.dot_general(rows, weight, (((1,), (1,)), ((), ())), preferred_element_type=f32)


def halo_gradients(delta, turned):
    fill = jnp.zeros((SLOT - S, C), f32)
    index = lax.broadcasted_iota(jnp.int32, (S, C), 0)

    def along_row(i):
        return [delta[pl.ds(PITCH * (i + 2) + 6 + t, 56), :] for t in range(3)]

    def along_column(j):
        return [delta[pl.ds(PITCH * t + 8 + j, 56, stride=PITCH), :] for t in range(3)]

    def block(a, b):
        return turned[:, C * (3 * a + b) : C * (3 * a + b) + C]

    sides = (
        (along_row(0), [block(2, t) for t in range(3)]),
        (along_column(S - 1), [block(t, 0) for t in range(3)]),
        (along_row(S - 1), [block(0, t) for t in range(3)]),
        (along_column(0), [block(t, 2) for t in range(3)]),
    )
    parts = []
    for lines, blocks in sides:
        full = dot_rows(
            jnp.concatenate(lines, axis=1).astype(bf16), jnp.concatenate(blocks, axis=1)
        )
        strip = full[1 : S + 1]
        strip = strip + jnp.where(index == 0, 0.5 * full[:1], 0.0)
        strip = strip + jnp.where(index == S - 1, 0.5 * full[S + 1 : S + 2], 0.0)
        parts += [strip, fill]
    return jnp.concatenate(parts, axis=0).astype(bf16)


def turn(weight, turned):
    for k in range(9):
        turned[:, C * k : C * k + C] = weight[8 - k]


def weight_gradient(delta, delta_t, wide, grad):
    view = delta.reshape(delta.shape[0] // PITCH, PITCH, C)
    for k in range(6):
        rows = view[pl.ds(2 + 8 * k, 8), pl.ds(8, S), :].reshape(8 * S, C)
        delta_t[:, 8 * S * k : 8 * S * (k + 1)] = rows.T.astype(bf16)

    def body(a, carry):
        flat = wide[pl.ds(a, S)].reshape(S * S, 3 * C)
        product = jnp.dot(delta_t[...], flat, preferred_element_type=f32)
        for b in range(3):
            grad[3 * a + b] = product[:, C * b : C * b + C].T
        return carry

    lax.fori_loop(0, 3, body, 0)


def field_gradient(wide, turned, grad):
    def body(k, carry):
        rows = pl.ds(pl.multiple_of(8 * S * k, 8 * S), 8 * S)
        grad[rows, :] = dot_rows(taps_of(wide, 8 * k), turned[...])
        return carry

    lax.fori_loop(0, 6, body, 0)


def add_strips(grad, strips):
    top, right, bottom, left = (strips[SLOT * s : SLOT * s + S] for s in range(4))
    grad[pl.ds(0, S), :] += top
    grad[pl.ds(S * (S - 1), S), :] += bottom
    grad[pl.ds(0, S, stride=S), :] += left
    grad[pl.ds(S - 1, S, stride=S), :] += right


def step_kernel(
    fields, weight_first, weight_second, neighbours, cotangent,
    out_field, grad_fields, first_out, second_out,
    padded, delta, wide_first, wide_second, wide_delta, delta_t, slope, grad,
    turned_first, turned_second, choose, place, outgoing, incoming, swap_sems,
    grad_first, grad_second, *reduce_scratch,
):
    me = Place()
    barrier = greet(me)
    half = len(REDUCE_SCRATCH)
    second_sum = Reduce(me, grad_second, *reduce_scratch[:half])
    first_sum = Reduce(me, grad_first, *reduce_scratch[half:])
    swaps = [Swap(me, outgoing.at[e], incoming.at[e], swap_sems.at[e]) for e in range(4)]

    routing(me, neighbours, choose, place)
    incoming[:, :, S:, :] = jnp.zeros((4, 4, SLOT - S, C), bf16)
    padded_view = padded.reshape(50, PITCH, C)
    delta_view = delta.reshape(58, PITCH, C)
    for r in (0, 1, 50, 51, 52, 53, 54, 55, 56, 57):
        delta_view[r] = jnp.zeros((PITCH, C), f32)
    delta_view[2:50, :8, :] = jnp.zeros((S, 8, C), f32)
    delta_view[2:50, 56:, :] = jnp.zeros((S, 8, C), f32)

    def load(k, carry):
        padded_view[pl.ds(1 + 8 * k, 8), pl.ds(8, S), :] = fields[pl.ds(8 * k, 8)].astype(f32)
        return carry

    lax.fori_loop(0, 6, load, 0)
    strips = edge_strips(padded, 1)
    pl.semaphore_wait(barrier, 40)
    swaps[0].send(strips, choose)
    spread(padded, 0, wide_first, 1, S)
    turn(weight_first, turned_first)
    turn(weight_second, turned_second)
    fill_halo(padded, swaps[0].receive(place), wide_first)

    def forward_first(k, carry):
        pre = jnp.dot(
            taps_of(wide_first, 8 * k),
            weight_first[...].reshape(9 * C, C),
            preferred_element_type=f32,
        )
        below = 0.5 * (1.0 + lax.erf(pre * root_half))
        rows = pl.ds(pl.multiple_of(8 * S * k, 8 * S), 8 * S)
        slope[rows, :] = below + pre * jnp.exp(-0.5 * pre * pre) * inv_root_tau
        hidden = (pre * below).astype(bf16).astype(f32)
        padded_view[pl.ds(1 + 8 * k, 8), pl.ds(8, S), :] = hidden.reshape(8, S, C)
        return carry

    lax.fori_loop(0, 6, forward_first, 0)
    swaps[1].send(edge_strips(padded, 1), choose)
    spread(padded, 0, wide_second, 1, S)
    fill_halo(padded, swaps[1].receive(place), wide_second)

    def forward_second(k, carry):
        pre = jnp.dot(
            taps_of(wide_second, 8 * k),
            weight_second[...].reshape(9 * C, C),
            preferred_element_type=f32,
        )
        below = 0.5 * (1.0 + lax.erf(pre * root_half))
        out_field[pl.ds(8 * k, 8)] = (pre * below).astype(bf16).reshape(8, S, C)
        steep = below + pre * jnp.exp(-0.5 * pre * pre) * inv_root_tau
        cot = cotangent[pl.ds(8 * k, 8)].astype(f32)
        error = (cot * steep.reshape(8, S, C)).astype(bf16).astype(f32)
        delta_view[pl.ds(2 + 8 * k, 8), pl.ds(8, S), :] = error
        return carry

    lax.fori_loop(0, 6, forward_second, 0)
    swaps[2].send(halo_gradients(delta, turned_second), choose)
    weight_gradient(delta, delta_t, wide_second, grad_second)
    second_sum.send_pair()
    spread(delta, 1, wide_delta, 0, 50)
    field_gradient(wide_delta, turned_second, grad)
    add_strips(grad, swaps[2].receive(place))

    def backward_first(k, carry):
        rows = pl.ds(pl.multiple_of(8 * S * k, 8 * S), 8 * S)
        error = (grad[rows, :] * slope[rows, :]).astype(bf16).astype(f32)
        delta_view[pl.ds(2 + 8 * k, 8), pl.ds(8, S), :] = error.reshape(8, S, C)
        return carry

    lax.fori_loop(0, 6, backward_first, 0)
    swaps[3].send(halo_gradients(delta, turned_first), choose)
    second_sum.send_plane()
    weight_gradient(delta, delta_t, wide_first, grad_first)
    first_sum.send_pair()
    spread(delta, 1, wide_delta, 0, 50)
    first_sum.send_plane()
    second_sum.send_column()
    field_gradient(wide_delta, turned_first, grad)
    add_strips(grad, swaps[3].receive(place))
    first_sum.send_column()
    second_sum.send_whole()

    def store(k, carry):
        rows = pl.ds(pl.multiple_of(8 * S * k, 8 * S), 8 * S)
        grad_fields[pl.ds(8 * k, 8)] = grad[rows, :].astype(bf16).reshape(8, S, C)
        return carry

    lax.fori_loop(0, 6, store, 0)
    first_sum.send_whole()
    second_sum.finish(second_out)
    first_sum.finish(first_out)
    for job in swaps + [first_sum, second_sum]:
        job.drain()


def local(fields, weight_first, weight_second, neighbours, cotangent):
    vmem = pl.BlockSpec(memory_space=pltpu.VMEM)
    smem = pl.BlockSpec(memory_space=pltpu.SMEM)
    tile = jax.ShapeDtypeStruct((S, S, C), bf16)
    sums = jax.ShapeDtypeStruct((9, C, C), f32)
    out_field, grad_fields, first, second = pl.pallas_call(
        step_kernel,
        out_shape=(tile, tile, sums, sums),
        in_specs=[vmem, vmem, vmem, smem, vmem],
        out_specs=(vmem, vmem, vmem, vmem),
        scratch_shapes=[
            pltpu.VMEM((50 * PITCH, C), f32),
            pltpu.VMEM((58 * PITCH, C), f32),
            pltpu.VMEM((50, S, 3 * C), bf16),
            pltpu.VMEM((50, S, 3 * C), bf16),
            pltpu.VMEM((50, S, 3 * C), bf16),
            pltpu.VMEM((C, S * S), bf16),
            pltpu.VMEM((S * S, C), f32),
            pltpu.VMEM((S * S, C), f32),
            pltpu.VMEM((C, 9 * C), bf16),
            pltpu.VMEM((C, 9 * C), bf16),
            pltpu.VMEM((4 * SLOT, 4 * SLOT), bf16),
            pltpu.VMEM((4 * SLOT, 4 * SLOT), bf16),
            pltpu.VMEM((4, 4, SLOT, C), bf16),
            pltpu.VMEM((4, 4, SLOT, C), bf16),
            pltpu.SemaphoreType.DMA((4, 2, 4)),
            pltpu.VMEM((9, C, C), f32),
            pltpu.VMEM((9, C, C), f32),
        ]
        + REDUCE_SCRATCH
        + REDUCE_SCRATCH,
        compiler_params=pltpu.CompilerParams(
            collective_id=0, has_side_effects=True, vmem_limit_bytes=60 * 1024 * 1024
        ),
    )(
        fields.reshape(S, S, C),
        weight_first.reshape(9, C, C),
        weight_second.reshape(9, C, C),
        neighbours,
        cotangent.reshape(S, S, C),
    )
    return (
        out_field[None, None],
        grad_fields[None, None],
        first.reshape(3, 3, C, C),
        second.reshape(3, 3, C, C),
    )


def solution(mesh):
    placed = (P("ens", "tile", None, None, None), P(), P(), P(), P("ens", "tile", None, None, None))
    return jax.shard_map(
        local,
        mesh=mesh,
        in_specs=placed,
        out_specs=(
            P("ens", "tile", None, None, None),
            P("ens", "tile", None, None, None),
            P(),
            P(),
        ),
        check_vma=False,
    )
```

profile of v0, /device:TPU:1, one launch (start us, length us, event | category | flops | bytes accessed | tf_op | source)
XLA Modules:
  0.0 69.3 jit_solution(8717013313196257479)
XLA Ops:
  0.6 0.0 copy-start.3
  0.6 0.7 copy-done.3
  1.3 0.7 %copy.9.neighbours = s32[128,4]{1,0:T(8,128)} copy(s32[128,4]{0,1:T(4,128)S(1)} %copy-done.3) | data formatting | bytes 4096 | tf_op args[3]
  2.1 61.9 %shard_map.84 = (bf16[48,48,128]{2,1,0:T(8,128)(2,1)}, bf16[48,48,128]{2,1,0:T(8,128)(2,1)}, f32[9,128,128]{2,1,0:T(8,128)}, f32[9,128,128]{2,1,0:T(8,128)}) custom-call(bf16[48,48,128]{2,1,0:T(8,128)(2,1)} %bitcast.8, bf16[9,128,128]{2,1,0:T(8,128)(2,1)} %bitcast.14, bf16[9,128,128]{2,1,0:T(8,128)(2,1)} %bitcast.15, s32[128,4]{1,0:T(8,128)} %copy.9.neighbours, ...), custom_call_target="tpu_custom_call" | custom-call | tf_op jit(solution)/shard_map/pallas_call | solution.py:530
  63.9 0.0 copy-start.2
  64.0 2.0 %copy.14 = bf16[1,1,48,48,128]{4,3,2,1,0:T(8,128)(2,1)} copy(bf16[1,1,48,48,128]{4,3,2,1,0:T(8,128)(2,1)} %bitcast.13) | data formatting | bytes 1179648
  65.9 0.0 copy-done.2
  65.9 0.0 copy-start.1
  65.9 0.8 %copy.15 = bf16[1,1,48,48,128]{4,3,2,1,0:T(8,128)(2,1)} copy(bf16[1,1,48,48,128]{4,3,2,1,0:T(8,128)(2,1)S(1)} %bitcast.12) | data formatting | bytes 1179648
  66.8 0.5 copy-done.1
  67.2 0.0 copy-start
  67.2 0.8 %copy.16 = f32[3,3,128,128]{3,2,1,0:T(8,128)} copy(f32[3,3,128,128]{3,2,1,0:T(8,128)S(1)} %bitcast.11) | data formatting | bytes 1179648
  68.0 0.5 copy-done
  68.5 0.8 %copy.17 = f32[3,3,128,128]{3,2,1,0:T(8,128)} copy(f32[3,3,128,128]{3,2,1,0:T(8,128)S(1)} %bitcast.10) | data formatting | bytes 1179648
Async XLA Ops:
  0.6 0.7 copy-start.3
  63.9 2.0 %copy-start.2 = (bf16[48,48,128]{2,1,0:T(8,128)(2,1)S(1)}, bf16[48,48,128]{2,1,0:T(8,128)(2,1)}, u32[]{:S(2)}) copy-start(bf16[48,48,128]{2,1,0:T(8,128)(2,1)} %get-tuple-element.9) | copy-start | bytes 1769476
  65.9 1.3 %copy-start.1 = (f32[9,128,128]{2,1,0:T(8,128)S(1)}, f32[9,128,128]{2,1,0:T(8,128)}, u32[]{:S(2)}) copy-start(f32[9,128,128]{2,1,0:T(8,128)} %get-tuple-element.10) | copy-start | bytes 1769476
  67.2 1.3 %copy-start = (f32[9,128,128]{2,1,0:T(8,128)S(1)}, f32[9,128,128]{2,1,0:T(8,128)}, u32[]{:S(2)}) copy-start(f32[9,128,128]{2,1,0:T(8,128)} %get-tuple-element.11) | copy-start | bytes 1769476
where the time goes:
time: 69.6 us; the launch traced here: 69.3 us
  Pallas kernels  61.9 us (89%)
  local copies, waits for them, and re-layouts  6.76 us (10%)
    pallas_call x1, Pallas kernels, local(): pl.pallas_call(step_kernel, out_shape=(tile, tile, sums, sums), in_specs=...  61.9 us
    unnamed x13, local copies, waits for them, and re-layouts  6.76 us

commit v1 on v0

v1 whole, which is shorter than its diff:
```python
import jax
import jax.numpy as jnp
from jax import lax
from jax.experimental import pallas as pl
from jax.experimental.pallas import tpu as pltpu
from jax.sharding import PartitionSpec as P

MESH = pl.DeviceIdType.MESH
root_half = 0.7071067811865476
inv_root_tau = 0.3989422804014327
f32, bf16 = jnp.float32, jnp.bfloat16
S, C = 48, 128
PITCH = 64
SLOT = 64
OFFSETS = (1, -1, 16, -16)


TAPS = 5


class Place:
    def __init__(self):
        ens = lax.axis_index("ens")
        tile = lax.axis_index("tile")
        self.tile = tile
        self.core = tile % 2
        self.z = ens * 4 + (tile // 2) % 4
        self.q = tile // 8

    def device(self, q, z, core):
        return {"ens": z // 4, "tile": q * 8 + (z % 4) * 2 + core}


def greet(me):
    barrier = pltpu.get_barrier_semaphore()

    def signal(target):
        pl.semaphore_signal(barrier, inc=1, device_id=target, device_id_type=MESH)

    def plane(r, carry):
        signal(me.device((me.q + r) % 16, me.z, me.core))
        signal(me.device((me.q + r) % 16, me.z, 1 - me.core))
        return carry

    signal(me.device(me.q, me.z, 1 - me.core))
    lax.fori_loop(1, 16, plane, 0)

    def column(r, carry):
        signal(me.device(me.q, (me.z + r) % 8, me.core))
        return carry

    lax.fori_loop(1, 8, column, 0)
    for step in (1, -1):
        signal({"tile": (me.tile + step) % 128})
    return barrier


class Reduce:
    def __init__(self, me, grad, pair_out, pair_in, part, plane_in, column_in, whole, sems):
        self.me, self.grad = me, grad
        self.pair_out, self.pair_in, self.part = pair_out, pair_in, part
        self.plane_in, self.column_in, self.whole = plane_in, column_in, whole
        self.sems = sems

    def pair_copy(self, part, core):
        slots = pl.ds(2 * (1 - core), 3) if part == 0 else pl.ds(3 * core, 2)
        me = self.me
        return pltpu.make_async_remote_copy(
            src_ref=self.pair_out.at[slots],
            dst_ref=self.pair_in.at[slots],
            send_sem=self.sems.at[0, part],
            recv_sem=self.sems.at[1, part],
            device_id=me.device(me.q, me.z, 1 - me.core),
            device_id_type=MESH,
        )

    def plane_copy(self, target, source):
        return pltpu.make_async_remote_copy(
            src_ref=self.part.at[target],
            dst_ref=self.plane_in.at[source],
            send_sem=self.sems.at[0, 2 + target],
            recv_sem=self.sems.at[1, 2 + source],
            device_id=self.me.device(target, self.me.z, self.me.core),
            device_id_type=MESH,
        )

    def column_copy(self, target, source):
        return pltpu.make_async_remote_copy(
            src_ref=self.column_in.at[source],
            dst_ref=self.column_in.at[source],
            send_sem=self.sems.at[0, 18 + target],
            recv_sem=self.sems.at[1, 18 + source],
            device_id=self.me.device(self.me.q, target, self.me.core),
            device_id_type=MESH,
        )

    def whole_copy(self, target, source):
        core = self.me.core
        return pltpu.make_async_remote_copy(
            src_ref=self.whole.at[core, source],
            dst_ref=self.whole.at[core, source],
            send_sem=self.sems.at[0, 26 + target],
            recv_sem=self.sems.at[1, 26 + source],
            device_id=self.me.device(target, self.me.z, core),
            device_id_type=MESH,
        )

    def relay_copy(self, source, core):
        me = self.me
        return pltpu.make_async_remote_copy(
            src_ref=self.whole.at[core, source],
            dst_ref=self.whole.at[core, source],
            send_sem=self.sems.at[0, 42 + source],
            recv_sem=self.sems.at[1, 42 + source],
            device_id=me.device(me.q, me.z, 1 - me.core),
            device_id_type=MESH,
        )

    def send_pair(self, part):
        core = self.me.core
        for u in range(3 - part):
            if part == 0:
                slot, tap = 2 * (1 - core) + u, 6 * (1 - core) + u
            else:
                slot, tap = 3 * core + u, 4 - core + u
            self.pair_out[slot] = self.grad[tap].astype(bf16)
        self.pair_copy(part, core).start()

    def send_plane(self):
        me = self.me
        for part in range(2):
            self.pair_copy(part, 1 - me.core).wait_recv()

        def band(m, carry):
            rows = pl.ds(pl.multiple_of(16 * m, 16), 16)
            for t in range(TAPS):
                total = self.grad[4 * me.core + t, rows, :] + self.pair_in[t, rows, :].astype(f32)
                self.part[2 * m, t] = total[:8].astype(bf16)
                self.part[2 * m + 1, t] = total[8:].astype(bf16)
            return carry

        lax.fori_loop(0, 8, band, 0)
        self.plane_in[me.q] = self.part[me.q]

        def send(r, carry):
            self.plane_copy((me.q + r) % 16, me.q).start()
            return carry

        lax.fori_loop(1, 16, send, 0)

    def send_column(self):
        me = self.me

        def wait(r, carry):
            self.plane_copy((me.q + r) % 16, (me.q + r) % 16).wait_recv()
            return carry

        lax.fori_loop(1, 16, wait, 0)
        for t in range(TAPS):
            total = self.plane_in[0, t].astype(f32)
            for k in range(1, 16):
                total = total + self.plane_in[k, t].astype(f32)
            self.column_in[me.z, t] = total.astype(bf16)

        def send(r, carry):
            self.column_copy((me.z + r) % 8, me.z).start()
            return carry

        lax.fori_loop(1, 8, send, 0)

    def send_whole(self):
        me = self.me

        def wait(r, carry):
            self.column_copy((me.z + r) % 8, (me.z + r) % 8).wait_recv()
            return carry

        lax.fori_loop(1, 8, wait, 0)
        for t in range(TAPS):
            total = self.column_in[0, t].astype(f32)
            for k in range(1, 8):
                total = total + self.column_in[k, t].astype(f32)
            self.whole[me.core, me.q, t] = total.astype(bf16)

        def send(r, carry):
            self.whole_copy((me.q + r) % 16, me.q).start()
            return carry

        lax.fori_loop(1, 16, send, 0)
        self.relay_copy(me.q, me.core).start()

    def relay(self):
        me = self.me

        def forward(r, carry):
            source = (me.q + r) % 16
            self.whole_copy(source, source).wait_recv()
            self.relay_copy(source, me.core).start()
            return carry

        lax.fori_loop(1, 16, forward, 0)

    def finish(self, out):
        me = self.me

        def wait(r, carry):
            self.relay_copy(r, 1 - me.core).wait_recv()
            return carry

        lax.fori_loop(0, 16, wait, 0)
        for tap in range(9):
            core = 0 if tap < TAPS else 1
            for k in range(16):
                out[tap, 8 * k : 8 * k + 8, :] = self.whole[core, k, tap - 4 * core].astype(
                    f32
                )

    def drain(self):
        me = self.me
        for part in range(2):
            self.pair_copy(part, me.core).wait_send()

        def plane(r, carry):
            target = (me.q + r) % 16
            self.plane_copy(target, me.q).wait_send()
            self.whole_copy(target, me.q).wait_send()
            self.relay_copy(target, me.core).wait_send()
            return carry

        lax.fori_loop(1, 16, plane, 0)
        self.relay_copy(me.q, me.core).wait_send()

        def column(r, carry):
            self.column_copy((me.z + r) % 8, me.z).wait_send()
            return carry

        lax.fori_loop(1, 8, column, 0)


REDUCE_SCRATCH = [
    pltpu.VMEM((TAPS, 128, 128), bf16),
    pltpu.VMEM((TAPS, 128, 128), bf16),
    pltpu.VMEM((16, TAPS, 8, 128), bf16),
    pltpu.VMEM((16, TAPS, 8, 128), bf16),
    pltpu.VMEM((8, TAPS, 8, 128), bf16),
    pltpu.VMEM((2, 16, TAPS, 8, 128), bf16),
    pltpu.SemaphoreType.DMA((2, 58)),
]


class Swap:
    def __init__(self, me, outgoing, incoming, sems):
        self.me, self.outgoing, self.incoming, self.sems = me, outgoing, incoming, sems

    def copy(self, d):
        return pltpu.make_async_remote_copy(
            src_ref=self.outgoing.at[d, pl.ds(0, S)],
            dst_ref=self.incoming.at[d ^ 1, pl.ds(0, S)],
            send_sem=self.sems.at[0, d],
            recv_sem=self.sems.at[1, d ^ 1],
            device_id={"tile": (self.me.tile + OFFSETS[d]) % 128},
            device_id_type=MESH,
        )

    def send(self, strips, choose):
        routed = jnp.dot(choose[...], strips, preferred_element_type=f32).astype(bf16)
        for d in range(4):
            self.outgoing[d] = routed[SLOT * d : SLOT * d + SLOT]
        for d in range(4):
            self.copy(d).start()

    def receive(self, place):
        for d in range(4):
            self.copy(d).wait_recv()
        return jnp.dot(
            place[...], self.incoming[...].reshape(4 * SLOT, C), preferred_element_type=f32
        )

    def drain(self):
        for d in range(4):
            self.copy(d).wait_send()


def routing(me, neighbours, choose, place):
    sides = []
    for offset in OFFSETS:
        target = (me.tile + offset) % 128
        side = jnp.int32(0)
        for s in range(1, 4):
            side = side + jnp.where(neighbours[s, me.tile] == target, s, 0)
        sides.append(side)
    row = lax.broadcasted_iota(jnp.int32, (256, 256), 0)
    col = lax.broadcasted_iota(jnp.int32, (256, 256), 1)
    i, j = row % SLOT, col % SLOT
    inside = (i < S) & (j < S)
    same, flip = inside & (i == j), inside & (i + j == S - 1)

    def side_of(direction):
        out = jnp.full((256, 256), sides[0], jnp.int32)
        for d in range(1, 4):
            out = jnp.where(direction == d, sides[d], out)
        return out

    side = col // SLOT
    hit = (side_of(row // SLOT) == side) & (((side < 2) & same) | ((side >= 2) & flip))
    choose[...] = jnp.where(hit, 1.0, 0.0).astype(bf16)
    side = row // SLOT
    hit = (side_of(col // SLOT) == side) & (((side < 2) & flip) | ((side >= 2) & same))
    place[...] = jnp.where(hit, 1.0, 0.0).astype(bf16)


def pack_strips(strips):
    fill = jnp.zeros((SLOT - S, C), f32)
    return jnp.concatenate(
        [part for strip in strips for part in (strip, fill)], axis=0
    ).astype(bf16)


def border(base, pitch, left):
    start = base * pitch + left
    return (
        pl.ds(start, S),
        pl.ds(start + S - 1, S, stride=pitch),
        pl.ds(start + (S - 1) * pitch, S),
        pl.ds(start, S, stride=pitch),
    )


FLAT = border(0, S, 0)
PADDED = border(1, PITCH, 8)
WIDER = border(2, PITCH, 8)


def spread(padded, base, wide, first, count):
    view = padded.reshape(padded.shape[0] // PITCH, PITCH, C)

    def body(k, carry):
        r = first + k
        for b in range(3):
            wide[r, :, C * b : C * b + C] = view[r + base, pl.ds(7 + b, S), :].astype(bf16)
        return carry

    lax.fori_loop(0, count, body, 0, unroll=4)


def write_ring(padded, halo):
    top, right, bottom, left = (halo[SLOT * s : SLOT * s + S] for s in range(4))
    padded[pl.ds(PITCH + 7, S, stride=PITCH), :] = left
    padded[pl.ds(PITCH + 56, S, stride=PITCH), :] = right
    padded[pl.ds(8, S), :] = top
    padded[pl.ds(PITCH * 49 + 8, S), :] = bottom

    def corner(row, col, one, two):
        padded[pl.ds(PITCH * row + col, 1), :] = (0.5 * (one + two)).astype(bf16).astype(f32)

    corner(0, 7, top[:1], left[:1])
    corner(0, 56, top[S - 1 :], right[:1])
    corner(49, 7, left[S - 1 :], bottom[:1])
    corner(49, 56, bottom[S - 1 :], right[S - 1 :])


def add_halo_terms(padded, weight, pre):
    index = lax.broadcasted_iota(jnp.int32, (S, C), 0)

    def along_row(r):
        return [padded[pl.ds(PITCH * r + 7 + t, S), :] for t in range(3)]

    def along_column(col):
        lines = [padded[pl.ds(PITCH * t + col, S, stride=PITCH), :] for t in range(3)]
        lines[0] = jnp.where(index == 0, 0.0, lines[0])
        lines[2] = jnp.where(index == S - 1, 0.0, lines[2])
        return lines

    sides = (
        (along_row(0), (0, 1, 2)),
        (along_column(56), (2, 5, 8)),
        (along_row(49), (6, 7, 8)),
        (along_column(7), (0, 3, 6)),
    )
    terms = [
        jnp.dot(
            jnp.concatenate(lines, axis=1).astype(bf16),
            jnp.concatenate([weight[t] for t in taps], axis=0),
            preferred_element_type=f32,
        )
        for lines, taps in sides
    ]
    for where, term in zip(FLAT, terms):
        pre[where, :] += term


def spread_halo(padded, wide):
    view = padded.reshape(50, PITCH, C)
    for r in (0, 49):
        for b in range(3):
            wide[r, :, C * b : C * b + C] = view[r, pl.ds(7 + b, S), :].astype(bf16)

    def body(k, carry):
        r = 1 + k
        wide[r, :16, :C] = view[r, pl.ds(7, 16), :].astype(bf16)
        wide[r, 32:, 2 * C :] = view[r, pl.ds(41, 16), :].astype(bf16)
        return carry

    lax.fori_loop(0, S, body, 0, unroll=4)


def clear_ring(padded, rows, first):
    view = padded.reshape(padded.shape[0] // PITCH, PITCH, C)
    for r in rows:
        view[r] = jnp.zeros((PITCH, C), f32)
    view[first : first + S, :8, :] = jnp.zeros((S, 8, C), f32)
    view[first : first + S, 56:, :] = jnp.zeros((S, 8, C), f32)


def gelu(pre):
    below = 0.5 * (1.0 + lax.erf(pre * root_half))
    return pre * below, below + pre * jnp.exp(-0.5 * pre * pre) * inv_root_tau


def rounded(value):
    return value.astype(bf16).astype(f32)


def block(k):
    return pl.ds(pl.multiple_of(8 * S * k, 8 * S), 8 * S)


def taps_of(wide, start):
    return jnp.concatenate(
        [wide[pl.ds(start + a, 8)].reshape(8 * S, 3 * C) for a in range(3)], axis=1
    )


def dot_rows(rows, weight):
    return lax.dot_general(rows, weight, (((1,), (1,)), ((), ())), preferred_element_type=f32)


def halo_gradients(delta, turned):
    index = lax.broadcasted_iota(jnp.int32, (S, C), 0)

    def along_row(i):
        return [delta[pl.ds(PITCH * (i + 2) + 6 + t, 56), :] for t in range(3)]

    def along_column(j):
        return [delta[pl.ds(PITCH * t + 8 + j, 56, stride=PITCH), :] for t in range(3)]

    def tap(a, b):
        return turned[:, C * (3 * a + b) : C * (3 * a + b) + C]

    sides = (
        (along_row(0), [tap(2, t) for t in range(3)]),
        (along_column(S - 1), [tap(t, 0) for t in range(3)]),
        (along_row(S - 1), [tap(0, t) for t in range(3)]),
        (along_column(0), [tap(t, 2) for t in range(3)]),
    )
    parts = []
    for lines, blocks in sides:
        full = dot_rows(
            jnp.concatenate(lines, axis=1).astype(bf16), jnp.concatenate(blocks, axis=1)
        )
        strip = full[1 : S + 1]
        strip = strip + jnp.where(index == 0, 0.5 * full[:1], 0.0)
        strip = strip + jnp.where(index == S - 1, 0.5 * full[S + 1 : S + 2], 0.0)
        parts.append(strip)
    return pack_strips(parts)


def turn(weight, turned):
    for k in range(9):
        turned[:, C * k : C * k + C] = weight[8 - k]


def weight_gradient(me, delta, delta_t, wide, total):
    view = delta.reshape(delta.shape[0] // PITCH, PITCH, C)
    for k in range(6):
        rows = view[pl.ds(2 + 8 * k, 8), pl.ds(8, S), :].reshape(8 * S, C)
        delta_t[:, 8 * S * k : 8 * S * (k + 1)] = rows.T.astype(bf16)

    def tap_row(i):
        a = (1 - me.core) * (2 - i) + me.core * i
        flat = wide[pl.ds(a, S)].reshape(S * S, 3 * C)
        product = jnp.dot(delta_t[...], flat, preferred_element_type=f32)
        for b in range(3):
            total.grad[3 * a + b] = product[:, C * b : C * b + C].T

    for i in range(3):
        tap_row(i)
        if i < 2:
            total.send_pair(i)


def field_gradient(wide, turned, grad):
    def body(k, carry):
        grad[block(k), :] = dot_rows(taps_of(wide, 8 * k), turned[...])
        return carry

    lax.fori_loop(0, 6, body, 0)


def add_strips(grad, strips):
    for s in range(4):
        grad[FLAT[s], :] += strips[SLOT * s : SLOT * s + S]


def step_kernel(
    fields_hbm, weight_first_hbm, weight_second_hbm, neighbours, cotangent_hbm,
    out_field, grad_fields, first_out, second_out,
    fields, weight_first, weight_second, cotangent, load_sems,
    padded_first, padded_second, delta, wide_first, wide_second, wide_delta, delta_t,
    pre, slope, value, grad,
    turned_first, turned_second, choose, place, outgoing, incoming, swap_sems,
    grad_first, grad_second, *reduce_scratch,
):
    loads = [
        pltpu.make_async_copy(source, target, load_sems.at[n])
        for n, (source, target) in enumerate(
            (
                (fields_hbm, fields),
                (weight_first_hbm, weight_first),
                (weight_second_hbm, weight_second),
                (cotangent_hbm, cotangent),
            )
        )
    ]
    for load in loads:
        load.start()
    me = Place()
    barrier = greet(me)
    half = len(REDUCE_SCRATCH)
    second_sum = Reduce(me, grad_second, *reduce_scratch[:half])
    first_sum = Reduce(me, grad_first, *reduce_scratch[half:])
    swaps = [Swap(me, outgoing.at[e], incoming.at[e], swap_sems.at[e]) for e in range(4)]

    routing(me, neighbours, choose, place)
    incoming[:, :, S:, :] = jnp.zeros((4, 4, SLOT - S, C), bf16)
    clear_ring(padded_first, (0, 49), 1)
    clear_ring(padded_second, (0, 49), 1)
    clear_ring(delta, (0, 1, 50, 51, 52, 53, 54, 55, 56, 57), 2)
    first_view = padded_first.reshape(50, PITCH, C)
    second_view = padded_second.reshape(50, PITCH, C)
    delta_view = delta.reshape(58, PITCH, C)
    loads[0].wait()

    def load_fields(k, carry):
        first_view[pl.ds(1 + 8 * k, 8), pl.ds(8, S), :] = fields[pl.ds(8 * k, 8)].astype(f32)
        return carry

    lax.fori_loop(0, 6, load_fields, 0)
    strips = pack_strips([padded_first[where, :] for where in PADDED])
    pl.semaphore_wait(barrier, 40)
    swaps[0].send(strips, choose)

    spread(padded_first, 0, wide_first, 0, 50)
    loads[1].wait()

    def forward_first(k, carry):
        now = jnp.dot(
            taps_of(wide_first, 8 * k),
            weight_first[...].reshape(9 * C, C),
            preferred_element_type=f32,
        )
        pre[block(k), :] = now
        hidden, steep = gelu(now)
        slope[block(k), :] = steep
        second_view[pl.ds(1 + 8 * k, 8), pl.ds(8, S), :] = rounded(hidden).reshape(8, S, C)
        return carry

    lax.fori_loop(0, 6, forward_first, 0)
    write_ring(padded_first, swaps[0].receive(place))
    add_halo_terms(padded_first, weight_first, pre)
    strips = []
    for s in range(4):
        hidden, steep = gelu(pre[FLAT[s], :])
        hidden = rounded(hidden)
        slope[FLAT[s], :] = steep
        padded_second[PADDED[s], :] = hidden
        strips.append(hidden)
    swaps[1].send(pack_strips(strips), choose)

    spread(padded_second, 0, wide_second, 0, 50)
    loads[2].wait()
    loads[3].wait()

    def forward_second(k, carry):
        now = jnp.dot(
            taps_of(wide_second, 8 * k),
            weight_second[...].reshape(9 * C, C),
            preferred_element_type=f32,
        )
        pre[block(k), :] = now
        out, steep = gelu(now)
        value[block(k), :] = out
        cot = cotangent[pl.ds(8 * k, 8)].astype(f32)
        grad[block(k), :] = cot.reshape(8 * S, C)
        error = cot * steep.reshape(8, S, C)
        delta_view[pl.ds(2 + 8 * k, 8), pl.ds(8, S), :] = rounded(error)
        return carry

    lax.fori_loop(0, 6, forward_second, 0)
    turn(weight_second, turned_second)
    turn(weight_first, turned_first)
    spread_halo(padded_first, wide_first)
    write_ring(padded_second, swaps[1].receive(place))
    add_halo_terms(padded_second, weight_second, pre)
    for s in range(4):
        out, steep = gelu(pre[FLAT[s], :])
        value[FLAT[s], :] = out
        delta[WIDER[s], :] = rounded(grad[FLAT[s], :] * steep)
    swaps[2].send(halo_gradients(delta, turned_second), choose)

    spread_halo(padded_second, wide_second)
    weight_gradient(me, delta, delta_t, wide_second, second_sum)
    spread(delta, 1, wide_delta, 0, 50)
    second_sum.send_plane()
    field_gradient(wide_delta, turned_second, grad)
    add_strips(grad, swaps[2].receive(place))

    def backward_first(k, carry):
        error = rounded(grad[block(k), :] * slope[block(k), :])
        delta_view[pl.ds(2 + 8 * k, 8), pl.ds(8, S), :] = error.reshape(8, S, C)
        return carry

    lax.fori_loop(0, 6, backward_first, 0)
    weight_gradient(me, delta, delta_t, wide_first, first_sum)
    swaps[3].send(halo_gradients(delta, turned_first), choose)
    first_sum.send_plane()
    second_sum.send_column()
    spread(delta, 1, wide_delta, 0, 50)
    field_gradient(wide_delta, turned_first, grad)
    add_strips(grad, swaps[3].receive(place))
    first_sum.send_column()
    second_sum.send_whole()

    def store(k, carry):
        grad_fields[pl.ds(8 * k, 8)] = grad[block(k), :].astype(bf16).reshape(8, S, C)
        out_field[pl.ds(8 * k, 8)] = value[block(k), :].astype(bf16).reshape(8, S, C)
        return carry

    lax.fori_loop(0, 6, store, 0)
    first_sum.send_whole()
    second_sum.relay()
    second_sum.finish(second_out)
    first_sum.relay()
    first_sum.finish(first_out)
    for job in swaps + [first_sum, second_sum]:
        job.drain()


def store_kernel(*refs):
    copies = [
        pltpu.make_async_copy(refs[n], refs[4 + n], refs[8].at[n]) for n in range(4)
    ]
    for copy in copies:
        copy.start()
    for copy in copies:
        copy.wait()


def local(fields, weight_first, weight_second, neighbours, cotangent):
    vmem = pl.BlockSpec(memory_space=pltpu.VMEM)
    smem = pl.BlockSpec(memory_space=pltpu.SMEM)
    hbm = pl.BlockSpec(memory_space=pltpu.HBM)
    tile = (S, S, C)
    sums = (9, C, C)
    results = pl.pallas_call(
        step_kernel,
        out_shape=(
            pltpu.VMEM(tile, bf16),
            pltpu.VMEM(tile, bf16),
            pltpu.VMEM(sums, f32),
            pltpu.VMEM(sums, f32),
        ),
        in_specs=[hbm, hbm, hbm, smem, hbm],
        out_specs=(vmem, vmem, vmem, vmem),
        scratch_shapes=[
            pltpu.VMEM(tile, bf16),
            pltpu.VMEM(sums, bf16),
            pltpu.VMEM(sums, bf16),
            pltpu.VMEM(tile, bf16),
            pltpu.SemaphoreType.DMA((4,)),
            pltpu.VMEM((50 * PITCH, C), f32),
            pltpu.VMEM((50 * PITCH, C), f32),
            pltpu.VMEM((58 * PITCH, C), f32),
            pltpu.VMEM((50, S, 3 * C), bf16),
            pltpu.VMEM((50, S, 3 * C), bf16),
            pltpu.VMEM((50, S, 3 * C), bf16),
            pltpu.VMEM((C, S * S), bf16),
            pltpu.VMEM((S * S, C), f32),
            pltpu.VMEM((S * S, C), f32),
            pltpu.VMEM((S * S, C), f32),
            pltpu.VMEM((S * S, C), f32),
            pltpu.VMEM((C, 9 * C), bf16),
            pltpu.VMEM((C, 9 * C), bf16),
            pltpu.VMEM((4 * SLOT, 4 * SLOT), bf16),
            pltpu.VMEM((4 * SLOT, 4 * SLOT), bf16),
            pltpu.VMEM((4, 4, SLOT, C), bf16),
            pltpu.VMEM((4, 4, SLOT, C), bf16),
            pltpu.SemaphoreType.DMA((4, 2, 4)),
            pltpu.VMEM(sums, f32),
            pltpu.VMEM(sums, f32),
        ]
        + REDUCE_SCRATCH
        + REDUCE_SCRATCH,
        compiler_params=pltpu.CompilerParams(
            collective_id=0, has_side_effects=True, vmem_limit_bytes=64_500_000
        ),
    )(
        fields.reshape(tile),
        weight_first.reshape(sums),
        weight_second.reshape(sums),
        neighbours.T,
        cotangent.reshape(tile),
    )
    out_field, grad_fields, first, second = pl.pallas_call(
        store_kernel,
        out_shape=(
            jax.ShapeDtypeStruct(tile, bf16),
            jax.ShapeDtypeStruct(tile, bf16),
            jax.ShapeDtypeStruct(sums, f32),
            jax.ShapeDtypeStruct(sums, f32),
        ),
        in_specs=[vmem, vmem, vmem, vmem],
        out_specs=(hbm, hbm, hbm, hbm),
        scratch_shapes=[pltpu.SemaphoreType.DMA((4,))],
        compiler_params=pltpu.CompilerParams(vmem_limit_bytes=1024 * 1024),
    )(*results)
    return (
        out_field[None, None],
        grad_fields[None, None],
        first.reshape(3, 3, C, C),
        second.reshape(3, 3, C, C),
    )


def solution(mesh):
    placed = (P("ens", "tile", None, None, None), P(), P(), P(), P("ens", "tile", None, None, None))
    return jax.shard_map(
        local,
        mesh=mesh,
        in_specs=placed,
        out_specs=(
            P("ens", "tile", None, None, None),
            P("ens", "tile", None, None, None),
            P(),
            P(),
        ),
        check_vma=False,
    )
```

time: 69.6 us -> 55.2 us (0.79)
  Pallas kernels: 61.9 us -> 54.4 us
  local copies, waits for them, and re-layouts: 6.76 us -> 0 us
    pallas_call x1 -> x2, Pallas kernels: 61.9 us -> 54.4 us  [the longest x1 53 us: local(): pl.pallas_call(step_kernel, out_shape=(pltpu.VMEM(tile, bf16), pltpu.VMEM...]
    unnamed x13 -> x0, local copies, waits for them, and re-layouts: 6.76 us -> none
where the time goes in v1:
time: 55.2 us; the launch traced here: 55.1 us
  Pallas kernels  54.4 us (99%)
  between operations  0.64 us (1%)
    pallas_call x1, Pallas kernels, local(): pl.pallas_call(step_kernel, out_shape=(pltpu.VMEM(tile, bf16), pltpu.VMEM...  53 us
    pallas_call x1, Pallas kernels, local(): pl.pallas_call(store_kernel, out_shape=(jax.ShapeDtypeStruct(tile, bf16),...  1.43 us

profile of v1, /device:TPU:1, one launch (start us, length us, event | category | flops | bytes accessed | tf_op | source)
XLA Modules:
  0.0 55.1 jit_solution(17711594152356926728)
XLA Ops:
  0.6 53.0 %shard_map.84 = (bf16[48,48,128]{2,1,0:T(8,128)(2,1)S(1)}, bf16[48,48,128]{2,1,0:T(8,128)(2,1)S(1)}, f32[9,128,128]{2,1,0:T(8,128)S(1)}, f32[9,128,128]{2,1,0:T(8,128)S(1)}) custom-call(bf16[48,48,128]{2,1,0:T(8,128)(2,1)} %bitcast.9, bf16[9,128,128]{2,1,0:T(8,128)(2,1)} %bitcast.11, bf16[9,128,128]{2,1,0:T(8,128)(2,1)} %bitcast.12, s32[4,128]{1,0:T(4,128)} %bitcast.13, ...), custom_call_target="tpu_custom_call" | custom-call | tf_op jit(solution)/shard_map/pallas_call | solution.py:665
  53.6 1.4 %shard_map.85 = (bf16[48,48,128]{2,1,0:T(8,128)(2,1)}, bf16[48,48,128]{2,1,0:T(8,128)(2,1)}, f32[9,128,128]{2,1,0:T(8,128)}, f32[9,128,128]{2,1,0:T(8,128)}) custom-call(bf16[48,48,128]{2,1,0:T(8,128)(2,1)S(1)} %get-tuple-element.12.refs_0_, bf16[48,48,128]{2,1,0:T(8,128)(2,1)S(1)} %get-tuple-element.13.refs_1_, ...), custom_call_target="tpu_custom_call" | custom-call | tf_op jit(solution)/shard_map/pallas_call | solution.py:714

commit v2 on v1

--- a/solution.py
+++ b/solution.py
@@ -16,6 +16,10 @@
 
 
 TAPS = 5
+FAR_FIRST = sorted(
+    ((dx, dy) for dx in range(4) for dy in range(4) if dx or dy),
+    key=lambda d: -(min(d[0], 4 - d[0]) + min(d[1], 4 - d[1])),
+)
 
 
 class Place:
@@ -26,6 +30,10 @@
         self.core = tile % 2
         self.z = ens * 4 + (tile // 2) % 4
         self.q = tile // 8
+
+    def plane(self):
+        x, y = self.q // 4, self.q % 4
+        return [((x + dx) % 4) * 4 + (y + dy) % 4 for dx, dy in FAR_FIRST]
 
     def device(self, q, z, core):
         return {"ens": z // 4, "tile": q * 8 + (z % 4) * 2 + core}
@@ -78,8 +86,8 @@
         return pltpu.make_async_remote_copy(
             src_ref=self.part.at[target],
             dst_ref=self.plane_in.at[source],
-            send_sem=self.sems.at[0, 2 + target],
-            recv_sem=self.sems.at[1, 2 + source],
+            send_sem=self.sems.at[0, 2],
+            recv_sem=self.sems.at[1, 2],
             device_id=self.me.device(target, self.me.z, self.me.core),
             device_id_type=MESH,
         )
@@ -88,8 +96,8 @@
         return pltpu.make_async_remote_copy(
             src_ref=self.column_in.at[source],
             dst_ref=self.column_in.at[source],
-            send_sem=self.sems.at[0, 18 + target],
-            recv_sem=self.sems.at[1, 18 + source],
+            send_sem=self.sems.at[0, 3],
+            recv_sem=self.sems.at[1, 3],
             device_id=self.me.device(self.me.q, target, self.me.core),
             device_id_type=MESH,
         )
@@ -99,22 +107,43 @@
         return pltpu.make_async_remote_copy(
             src_ref=self.whole.at[core, source],
             dst_ref=self.whole.at[core, source],
-            send_sem=self.sems.at[0, 26 + target],
-            recv_sem=self.sems.at[1, 26 + source],
+            send_sem=self.sems.at[0, 4],
+            recv_sem=self.sems.at[1, 4],
             device_id=self.me.device(target, self.me.z, core),
             device_id_type=MESH,
         )
 
-    def relay_copy(self, source, core):
+    def relay_copy(self, core):
         me = self.me
         return pltpu.make_async_remote_copy(
-            src_ref=self.whole.at[core, source],
-            dst_ref=self.whole.at[core, source],
-            send_sem=self.sems.at[0, 42 + source],
-            recv_sem=self.sems.at[1, 42 + source],
+            src_ref=self.whole.at[core],
+            dst_ref=self.whole.at[core],
+            send_sem=self.sems.at[0, 5],
+            recv_sem=self.sems.at[1, 5],
             device_id=me.device(me.q, me.z, 1 - me.core),
             device_id_type=MESH,
         )
+
+    def stage(self, source, target, index):
+        me = self.me
+        return pltpu.make_async_remote_copy(
+            src_ref=source,
+            dst_ref=target,
+            send_sem=self.sems.at[0, index],
+            recv_sem=self.sems.at[1, index],
+            device_id=me.device(me.q, me.z, 1 - me.core),
+            device_id_type=MESH,
+        )
+
+    def plane_stage(self):
+        return self.stage(self.part.at[pl.ds(0, 15)], self.plane_in.at[pl.ds(0, 15)], 2)
+
+    def column_stage(self):
+        return self.stage(self.column_in.at[pl.ds(0, 7)], self.column_in.at[pl.ds(0, 7)], 3)
+
+    def whole_stage(self):
+        blocks = self.whole.at[self.me.core, pl.ds(0, 15)]
+        return self.stage(blocks, blocks, 4)
 
     def send_pair(self, part):
         core = self.me.core
@@ -142,99 +171,65 @@
         lax.fori_loop(0, 8, band, 0)
         self.plane_in[me.q] = self.part[me.q]
 
-        def send(r, carry):
-            self.plane_copy((me.q + r) % 16, me.q).start()
-            return carry
-
-        lax.fori_loop(1, 16, send, 0)
+        for target in me.plane():
+            self.plane_copy(target, me.q).start()
 
     def send_column(self):
         me = self.me
-
-        def wait(r, carry):
-            self.plane_copy((me.q + r) % 16, (me.q + r) % 16).wait_recv()
-            return carry
-
-        lax.fori_loop(1, 16, wait, 0)
+        self.plane_stage().wait_recv()
         for t in range(TAPS):
             total = self.plane_in[0, t].astype(f32)
             for k in range(1, 16):
                 total = total + self.plane_in[k, t].astype(f32)
             self.column_in[me.z, t] = total.astype(bf16)
 
-        def send(r, carry):
+        for r in (4, 3, 5, 2, 6, 1, 7):
             self.column_copy((me.z + r) % 8, me.z).start()
-            return carry
-
-        lax.fori_loop(1, 8, send, 0)
 
     def send_whole(self):
         me = self.me
-
-        def wait(r, carry):
-            self.column_copy((me.z + r) % 8, (me.z + r) % 8).wait_recv()
-            return carry
-
-        lax.fori_loop(1, 8, wait, 0)
+        self.column_stage().wait_recv()
         for t in range(TAPS):
             total = self.column_in[0, t].astype(f32)
             for k in range(1, 8):
                 total = total + self.column_in[k, t].astype(f32)
             self.whole[me.core, me.q, t] = total.astype(bf16)
 
-        def send(r, carry):
-            self.whole_copy((me.q + r) % 16, me.q).start()
+        for target in me.plane():
+            self.whole_copy(target, me.q).start()
+
+    def relay(self):
+        self.whole_stage().wait_recv()
+        self.relay_copy(self.me.core).start()
+
+    def finish(self, out, core):
+        def body(k, carry):
+            rows = pl.ds(pl.multiple_of(8 * k, 8), 8)
+            for u in range(4):
+                out[5 * core + u, rows, :] = self.whole[core, k, core + u].astype(f32)
             return carry
 
-        lax.fori_loop(1, 16, send, 0)
-        self.relay_copy(me.q, me.core).start()
-
-    def relay(self):
+        lax.fori_loop(0, 16, body, 0, unroll=4)
+
+    def finish_own(self, out):
+        self.finish(out, self.me.core)
+
+    def finish_other(self, out):
         me = self.me
 
-        def forward(r, carry):
-            source = (me.q + r) % 16
-            self.whole_copy(source, source).wait_recv()
-            self.relay_copy(source, me.core).start()
-            return carry
-
-        lax.fori_loop(1, 16, forward, 0)
-
-    def finish(self, out):
-        me = self.me
-
-        def wait(r, carry):
-            self.relay_copy(r, 1 - me.core).wait_recv()
-            return carry
-
-        lax.fori_loop(0, 16, wait, 0)
-        for tap in range(9):
-            core = 0 if tap < TAPS else 1
-            for k in range(16):
-                out[tap, 8 * k : 8 * k + 8, :] = self.whole[core, k, tap - 4 * core].astype(
-                    f32
-                )
+        self.relay_copy(1 - me.core).wait_recv()
+        self.finish(out, 1 - me.core)
+        for k in range(16):
+            out[4, 8 * k : 8 * k + 8, :] = self.whole[0, k, 4].astype(f32)
 
     def drain(self):
         me = self.me
         for part in range(2):
             self.pair_copy(part, me.core).wait_send()
-
-        def plane(r, carry):
-            target = (me.q + r) % 16
-            self.plane_copy(target, me.q).wait_send()
-            self.whole_copy(target, me.q).wait_send()
-            self.relay_copy(target, me.core).wait_send()
-            return carry
-
-        lax.fori_loop(1, 16, plane, 0)
-        self.relay_copy(me.q, me.core).wait_send()
-
-        def column(r, carry):
-            self.column_copy((me.z + r) % 8, me.z).wait_send()
-            return carry
-
-        lax.fori_loop(1, 8, column, 0)
+        self.plane_stage().wait_send()
+        self.column_stage().wait_send()
+        self.whole_stage().wait_send()
+        self.relay_copy(me.core).wait_send()
 
 
 REDUCE_SCRATCH = [
@@ -244,7 +239,7 @@
     pltpu.VMEM((16, TAPS, 8, 128), bf16),
     pltpu.VMEM((8, TAPS, 8, 128), bf16),
     pltpu.VMEM((2, 16, TAPS, 8, 128), bf16),
-    pltpu.SemaphoreType.DMA((2, 58)),
+    pltpu.SemaphoreType.DMA((2, 6)),
 ]
 
 
@@ -256,8 +251,8 @@
         return pltpu.make_async_remote_copy(
             src_ref=self.outgoing.at[d, pl.ds(0, S)],
             dst_ref=self.incoming.at[d ^ 1, pl.ds(0, S)],
-            send_sem=self.sems.at[0, d],
-            recv_sem=self.sems.at[1, d ^ 1],
+            send_sem=self.sems.at[0],
+            recv_sem=self.sems.at[1],
             device_id={"tile": (self.me.tile + OFFSETS[d]) % 128},
             device_id_type=MESH,
         )
@@ -270,15 +265,23 @@
             self.copy(d).start()
 
     def receive(self, place):
-        for d in range(4):
-            self.copy(d).wait_recv()
+        self.everything().wait_recv()
         return jnp.dot(
             place[...], self.incoming[...].reshape(4 * SLOT, C), preferred_element_type=f32
         )
 
+    def everything(self):
+        return pltpu.make_async_remote_copy(
+            src_ref=self.outgoing.at[:, pl.ds(0, S)],
+            dst_ref=self.incoming.at[:, pl.ds(0, S)],
+            send_sem=self.sems.at[0],
+            recv_sem=self.sems.at[1],
+            device_id={"tile": (self.me.tile + 1) % 128},
+            device_id_type=MESH,
+        )
+
     def drain(self):
-        for d in range(4):
-            self.copy(d).wait_send()
+        self.everything().wait_send()
 
 
 def routing(me, neighbours, choose, place):
@@ -624,24 +627,31 @@
     weight_gradient(me, delta, delta_t, wide_first, first_sum)
     swaps[3].send(halo_gradients(delta, turned_first), choose)
     first_sum.send_plane()
-    second_sum.send_column()
     spread(delta, 1, wide_delta, 0, 50)
     field_gradient(wide_delta, turned_first, grad)
-    add_strips(grad, swaps[3].receive(place))
+    second_sum.send_column()
+
+    def store_out(k, carry):
+        out_field[pl.ds(8 * k, 8)] = value[block(k), :].astype(bf16).reshape(8, S, C)
+        return carry
+
+    lax.fori_loop(0, 6, store_out, 0)
     first_sum.send_column()
     second_sum.send_whole()
-
-    def store(k, carry):
+    add_strips(grad, swaps[3].receive(place))
+
+    def store_grad(k, carry):
         grad_fields[pl.ds(8 * k, 8)] = grad[block(k), :].astype(bf16).reshape(8, S, C)
-        out_field[pl.ds(8 * k, 8)] = value[block(k), :].astype(bf16).reshape(8, S, C)
-        return carry
-
-    lax.fori_loop(0, 6, store, 0)
+        return carry
+
+    lax.fori_loop(0, 6, store_grad, 0)
     first_sum.send_whole()
     second_sum.relay()
-    second_sum.finish(second_out)
+    second_sum.finish_own(second_out)
+    second_sum.finish_other(second_out)
     first_sum.relay()
-    first_sum.finish(first_out)
+    first_sum.finish_own(first_out)
+    first_sum.finish_other(first_out)
     for job in swaps + [first_sum, second_sum]:
         job.drain()
 
@@ -695,7 +705,7 @@
             pltpu.VMEM((4 * SLOT, 4 * SLOT), bf16),
             pltpu.VMEM((4, 4, SLOT, C), bf16),
             pltpu.VMEM((4, 4, SLOT, C), bf16),
-            pltpu.SemaphoreType.DMA((4, 2, 4)),
+            pltpu.SemaphoreType.DMA((4, 2)),
             pltpu.VMEM(sums, f32),
             pltpu.VMEM(sums, f32),
         ]

time: 55.2 us -> 51.3 us (0.929)
  Pallas kernels: 54.4 us -> 50.5 us
    pallas_call x1, Pallas kernels: 53 us -> 49.1 us  [local(): pl.pallas_call(step_kernel, out_shape=(pltpu.VMEM(tile, bf16), pltpu.VMEM...]
where the time goes in v2:
time: 51.3 us; the launch traced here: 51.1 us
  Pallas kernels  50.5 us (98%)
  between operations  0.64 us (1%)
    pallas_call x1, Pallas kernels, local(): pl.pallas_call(step_kernel, out_shape=(pltpu.VMEM(tile, bf16), pltpu.VMEM...  49.1 us
    pallas_call x1, Pallas kernels, local(): pl.pallas_call(store_kernel, out_shape=(jax.ShapeDtypeStruct(tile, bf16),...  1.43 us

profile of v2, /device:TPU:1, one launch (start us, length us, event | category | flops | bytes accessed | tf_op | source)
XLA Modules:
  0.0 51.1 jit_solution(16138133190864752544)
XLA Ops:
  0.6 49.1 %shard_map.84 = (bf16[48,48,128]{2,1,0:T(8,128)(2,1)S(1)}, bf16[48,48,128]{2,1,0:T(8,128)(2,1)S(1)}, f32[9,128,128]{2,1,0:T(8,128)S(1)}, f32[9,128,128]{2,1,0:T(8,128)S(1)}) custom-call(bf16[48,48,128]{2,1,0:T(8,128)(2,1)} %bitcast.9, bf16[9,128,128]{2,1,0:T(8,128)(2,1)} %bitcast.11, bf16[9,128,128]{2,1,0:T(8,128)(2,1)} %bitcast.12, s32[4,128]{1,0:T(4,128)} %bitcast.13, ...), custom_call_target="tpu_custom_call" | custom-call | tf_op jit(solution)/shard_map/pallas_call | solution.py:675
  49.7 1.4 %shard_map.85 = (bf16[48,48,128]{2,1,0:T(8,128)(2,1)}, bf16[48,48,128]{2,1,0:T(8,128)(2,1)}, f32[9,128,128]{2,1,0:T(8,128)}, f32[9,128,128]{2,1,0:T(8,128)}) custom-call(bf16[48,48,128]{2,1,0:T(8,128)(2,1)S(1)} %get-tuple-element.12.refs_0_, bf16[48,48,128]{2,1,0:T(8,128)(2,1)S(1)} %get-tuple-element.13.refs_1_, ...), custom_call_target="tpu_custom_call" | custom-call | tf_op jit(solution)/shard_map/pallas_call | solution.py:724

commit v3 on v2

--- a/solution.py
+++ b/solution.py
@@ -45,21 +45,13 @@
     def signal(target):
         pl.semaphore_signal(barrier, inc=1, device_id=target, device_id_type=MESH)
 
-    def plane(r, carry):
-        signal(me.device((me.q + r) % 16, me.z, me.core))
-        signal(me.device((me.q + r) % 16, me.z, 1 - me.core))
-        return carry
-
-    signal(me.device(me.q, me.z, 1 - me.core))
-    lax.fori_loop(1, 16, plane, 0)
-
-    def column(r, carry):
-        signal(me.device(me.q, (me.z + r) % 8, me.core))
-        return carry
-
-    lax.fori_loop(1, 8, column, 0)
     for step in (1, -1):
         signal({"tile": (me.tile + step) % 128})
+    for r in (4, 3, 5, 2, 6, 1, 7):
+        signal(me.device(me.q, (me.z + r) % 8, me.core))
+    for target in me.plane():
+        signal(me.device(target, me.z, me.core))
+    signal(me.device(me.q, me.z, 1 - me.core))
     return barrier
 
 
@@ -525,10 +517,10 @@
             )
         )
     ]
+    me = Place()
+    barrier = greet(me)
     for load in loads:
         load.start()
-    me = Place()
-    barrier = greet(me)
     half = len(REDUCE_SCRATCH)
     second_sum = Reduce(me, grad_second, *reduce_scratch[:half])
     first_sum = Reduce(me, grad_first, *reduce_scratch[half:])
@@ -550,7 +542,7 @@
 
     lax.fori_loop(0, 6, load_fields, 0)
     strips = pack_strips([padded_first[where, :] for where in PADDED])
-    pl.semaphore_wait(barrier, 40)
+    pl.semaphore_wait(barrier, 25)
     swaps[0].send(strips, choose)
 
     spread(padded_first, 0, wide_first, 0, 50)

time: 51.3 us -> 50.5 us (0.984)
  Pallas kernels: 50.5 us -> 49.7 us
    pallas_call x1, Pallas kernels: 49.1 us -> 48.3 us  [local(): pl.pallas_call(step_kernel, out_shape=(pltpu.VMEM(tile, bf16), pltpu.VMEM...]
where the time goes in v3:
time: 50.5 us; the launch traced here: 50.4 us
  Pallas kernels  49.7 us (98%)
  between operations  0.64 us (1%)
    pallas_call x1, Pallas kernels, local(): pl.pallas_call(step_kernel, out_shape=(pltpu.VMEM(tile, bf16), pltpu.VMEM...  48.3 us
    pallas_call x1, Pallas kernels, local(): pl.pallas_call(store_kernel, out_shape=(jax.ShapeDtypeStruct(tile, bf16),...  1.43 us

profile of v3, /device:TPU:1, one launch (start us, length us, event | category | flops | bytes accessed | tf_op | source)
XLA Modules:
  0.0 50.4 jit_solution(6905279507583993587)
XLA Ops:
  0.6 48.3 %shard_map.84 = (bf16[48,48,128]{2,1,0:T(8,128)(2,1)S(1)}, bf16[48,48,128]{2,1,0:T(8,128)(2,1)S(1)}, f32[9,128,128]{2,1,0:T(8,128)S(1)}, f32[9,128,128]{2,1,0:T(8,128)S(1)}) custom-call(bf16[48,48,128]{2,1,0:T(8,128)(2,1)} %bitcast.9, bf16[9,128,128]{2,1,0:T(8,128)(2,1)} %bitcast.11, bf16[9,128,128]{2,1,0:T(8,128)(2,1)} %bitcast.12, s32[4,128]{1,0:T(4,128)} %bitcast.13, ...), custom_call_target="tpu_custom_call" | custom-call | tf_op jit(solution)/shard_map/pallas_call | solution.py:667
  48.9 1.4 %shard_map.85 = (bf16[48,48,128]{2,1,0:T(8,128)(2,1)}, bf16[48,48,128]{2,1,0:T(8,128)(2,1)}, f32[9,128,128]{2,1,0:T(8,128)}, f32[9,128,128]{2,1,0:T(8,128)}) custom-call(bf16[48,48,128]{2,1,0:T(8,128)(2,1)S(1)} %get-tuple-element.12.refs_0_, bf16[48,48,128]{2,1,0:T(8,128)(2,1)S(1)} %get-tuple-element.13.refs_1_, ...), custom_call_target="tpu_custom_call" | custom-call | tf_op jit(solution)/shard_map/pallas_call | solution.py:716

commit v4 on v3

--- a/solution.py
+++ b/solution.py
@@ -16,6 +16,7 @@
 
 
 TAPS = 5
+FAR = 5
 FAR_FIRST = sorted(
     ((dx, dy) for dx in range(4) for dy in range(4) if dx or dy),
     key=lambda d: -(min(d[0], 4 - d[0]) + min(d[1], 4 - d[1])),
@@ -51,6 +52,8 @@
         signal(me.device(me.q, (me.z + r) % 8, me.core))
     for target in me.plane():
         signal(me.device(target, me.z, me.core))
+    for target in me.plane()[:FAR]:
+        signal(me.device(target, me.z, 1 - me.core))
     signal(me.device(me.q, me.z, 1 - me.core))
     return barrier
 
@@ -94,27 +97,20 @@
             device_id_type=MESH,
         )
 
-    def whole_copy(self, target, source):
-        core = self.me.core
-        return pltpu.make_async_remote_copy(
-            src_ref=self.whole.at[core, source],
-            dst_ref=self.whole.at[core, source],
-            send_sem=self.sems.at[0, 4],
-            recv_sem=self.sems.at[1, 4],
-            device_id=self.me.device(target, self.me.z, core),
-            device_id_type=MESH,
-        )
-
-    def relay_copy(self, core):
+    def whole_copy(self, target, target_core, index):
         me = self.me
         return pltpu.make_async_remote_copy(
-            src_ref=self.whole.at[core],
-            dst_ref=self.whole.at[core],
-            send_sem=self.sems.at[0, 5],
-            recv_sem=self.sems.at[1, 5],
-            device_id=me.device(me.q, me.z, 1 - me.core),
+            src_ref=self.whole.at[me.core, me.q],
+            dst_ref=self.whole.at[me.core, me.q],
+            send_sem=self.sems.at[0, index],
+            recv_sem=self.sems.at[1, index],
+            device_id=me.device(target, me.z, target_core),
             device_id_type=MESH,
         )
+
+    def relay_copy(self, source):
+        block = self.whole.at[self.me.core, source]
+        return self.stage(block, block, 5)
 
     def stage(self, source, target, index):
         me = self.me
@@ -133,9 +129,9 @@
     def column_stage(self):
         return self.stage(self.column_in.at[pl.ds(0, 7)], self.column_in.at[pl.ds(0, 7)], 3)
 
-    def whole_stage(self):
-        blocks = self.whole.at[self.me.core, pl.ds(0, 15)]
-        return self.stage(blocks, blocks, 4)
+    def whole_stage(self, index, count):
+        blocks = self.whole.at[0, pl.ds(0, count)]
+        return self.stage(blocks, blocks, index)
 
     def send_pair(self, part):
         core = self.me.core
@@ -187,12 +183,17 @@
                 total = total + self.column_in[k, t].astype(f32)
             self.whole[me.core, me.q, t] = total.astype(bf16)
 
-        for target in me.plane():
-            self.whole_copy(target, me.q).start()
+        for n, target in enumerate(me.plane()):
+            self.whole_copy(target, me.core, 4 if n < FAR else 7).start()
+            if n < FAR:
+                self.whole_copy(target, 1 - me.core, 6).start()
+        self.relay_copy(me.q).start()
 
     def relay(self):
-        self.whole_stage().wait_recv()
-        self.relay_copy(self.me.core).start()
+        self.whole_stage(7, 15 - FAR).wait_recv()
+        for source in self.me.plane()[FAR:]:
+            self.relay_copy(source).start()
+        self.whole_stage(4, FAR).wait_recv()
 
     def finish(self, out, core):
         def body(k, carry):
@@ -209,7 +210,8 @@
     def finish_other(self, out):
         me = self.me
 
-        self.relay_copy(1 - me.core).wait_recv()
+        self.whole_stage(6, FAR).wait_recv()
+        self.whole_stage(5, 16 - FAR).wait_recv()
         self.finish(out, 1 - me.core)
         for k in range(16):
             out[4, 8 * k : 8 * k + 8, :] = self.whole[0, k, 4].astype(f32)
@@ -220,8 +222,8 @@
             self.pair_copy(part, me.core).wait_send()
         self.plane_stage().wait_send()
         self.column_stage().wait_send()
-        self.whole_stage().wait_send()
-        self.relay_copy(me.core).wait_send()
+        for index, count in ((4, FAR), (5, 16 - FAR), (6, FAR), (7, 15 - FAR)):
+            self.whole_stage(index, count).wait_send()
 
 
 REDUCE_SCRATCH = [
@@ -231,7 +233,7 @@
     pltpu.VMEM((16, TAPS, 8, 128), bf16),
     pltpu.VMEM((8, TAPS, 8, 128), bf16),
     pltpu.VMEM((2, 16, TAPS, 8, 128), bf16),
-    pltpu.SemaphoreType.DMA((2, 6)),
+    pltpu.SemaphoreType.DMA((2, 8)),
 ]
 
 
@@ -542,7 +544,7 @@
 
     lax.fori_loop(0, 6, load_fields, 0)
     strips = pack_strips([padded_first[where, :] for where in PADDED])
-    pl.semaphore_wait(barrier, 25)
+    pl.semaphore_wait(barrier, 25 + FAR)
     swaps[0].send(strips, choose)
 
     spread(padded_first, 0, wide_first, 0, 50)

time: 50.5 us -> 50.3 us (level)
  no operation moved by 1% of the time
where the time goes in v4:
time: 50.3 us; the launch traced here: 50.2 us
  Pallas kernels  49.6 us (99%)
  between operations  0.64 us (1%)
    pallas_call x1, Pallas kernels, local(): pl.pallas_call(step_kernel, out_shape=(pltpu.VMEM(tile, bf16), pltpu.VMEM...  48.1 us
    pallas_call x1, Pallas kernels, local(): pl.pallas_call(store_kernel, out_shape=(jax.ShapeDtypeStruct(tile, bf16),...  1.43 us

profile of v4, /device:TPU:1, one launch (start us, length us, event | category | flops | bytes accessed | tf_op | source)
XLA Modules:
  0.0 50.2 jit_solution(17321684435584178971)
XLA Ops:
  0.6 48.1 %shard_map.84 = (bf16[48,48,128]{2,1,0:T(8,128)(2,1)S(1)}, bf16[48,48,128]{2,1,0:T(8,128)(2,1)S(1)}, f32[9,128,128]{2,1,0:T(8,128)S(1)}, f32[9,128,128]{2,1,0:T(8,128)S(1)}) custom-call(bf16[48,48,128]{2,1,0:T(8,128)(2,1)} %bitcast.9, bf16[9,128,128]{2,1,0:T(8,128)(2,1)} %bitcast.11, bf16[9,128,128]{2,1,0:T(8,128)(2,1)} %bitcast.12, s32[4,128]{1,0:T(4,128)} %bitcast.13, ...), custom_call_target="tpu_custom_call" | custom-call | tf_op jit(solution)/shard_map/pallas_call | solution.py:669
  48.8 1.4 %shard_map.85 = (bf16[48,48,128]{2,1,0:T(8,128)(2,1)}, bf16[48,48,128]{2,1,0:T(8,128)(2,1)}, f32[9,128,128]{2,1,0:T(8,128)}, f32[9,128,128]{2,1,0:T(8,128)}) custom-call(bf16[48,48,128]{2,1,0:T(8,128)(2,1)S(1)} %get-tuple-element.12.refs_0_, bf16[48,48,128]{2,1,0:T(8,128)(2,1)S(1)} %get-tuple-element.13.refs_1_, ...), custom_call_target="tpu_custom_call" | custom-call | tf_op jit(solution)/shard_map/pallas_call | solution.py:718
